TPU v7x, 32 devices: a whole 2x2x4 slice. The times are simulated.
32 devices in a mesh: role: 2 (over core), grp: 4 (over y, x), dev: 4 (over z).
Axes of the slice: x: 2, y: 2, z: 4, core: 2. Of those that a mesh axis runs over, the one named last changes fastest.
Arguments:
- tokens: bfloat16 [768, 2048], P(('role', 'grp', 'dev')), may hold values from -6 to 6
- norm_gain: float32 [2048], replicated, may hold values from 0.1 to 1.9
- q_gain: float32 [128], replicated, may hold values from 0.1 to 1.9
- k_gain: float32 [128], replicated, may hold values from 0.1 to 1.9
- post_gain: float32 [2048], replicated, may hold values from 0.1 to 1.9
- w_query: bfloat16 [2048, 4096], P(None, 'dev'), may hold values from -0.125 to 0.125
- w_keyvalue: bfloat16 [2048, 1024], P(None, 'dev'), may hold values from -0.125 to 0.125
- w_out: bfloat16 [4096, 2048], P('dev'), may hold values from -0.09375 to 0.09375
- cache_keys: bfloat16 [768, 4, 128, 128], P(('role', 'grp', 'dev')), may hold values from -400 to 400
- cache_values: bfloat16 [768, 4, 128, 128], P(('role', 'grp', 'dev')), may hold values from -6 to 6
- lengths: int32 [768], P(('role', 'grp', 'dev')), may hold values from 1 to 128
- expert_ids: int32 [768, 8], P(('role', 'grp', 'dev')), may hold values from 0 to 15, all different within a row; in each aligned block of 24 rows (0 to 23, 24 to 47, ...) at most 13 rows name the same one
- w_gate: bfloat16 [16, 2048, 768], P(('grp', 'dev'), None, 'role'), may hold values from -0.125 to 0.125
- w_up: bfloat16 [16, 2048, 768], P(('grp', 'dev'), None, 'role'), may hold values from -0.125 to 0.125
- w_down: bfloat16 [16, 768, 2048], P(('grp', 'dev'), 'role'), may hold values from -0.21875 to 0.21875
Outputs:
- layer_out: bfloat16 [768, 2048], P(('role', 'grp', 'dev'))
Inputs may be any that keep to these rules, and one draw needn't show every extreme that they name: `expert_ids`: each row names 8 different experts. Among the 24 rows of one device no expert is named more than 13 times; in the rows of some devices one expert is named exactly 13 times.
All inputs are finite; a program needn't handle non-finite values.
Results may differ from a plain program's by a relative error of at most 0.0099.
Values may be sent and summed in bfloat16 or wider, within the bound.
No kernel may reach another device: no remote copies, remote signals or barrier semaphores. Data moves between devices by JAX's collectives and lax.ppermute only.
A program may use at most 128 MiB of HBM per device.

v0:
```python
import jax
import jax.numpy as jnp
from jax import lax
from jax.sharding import PartitionSpec as P

epsilon = 1e-06
rope_base = 1000000.0


def rms_scale(values, gain):
    widened = values.astype(jnp.float32)
    mean_square = jnp.mean(widened * widened, axis=-1, keepdims=True)
    return widened * lax.rsqrt(mean_square + epsilon) * gain


def rotate(values, positions):
    half_dim = values.shape[-1] // 2
    frequency = rope_base ** (-jnp.arange(half_dim, dtype=jnp.float32) / half_dim)
    angles = positions.astype(jnp.float32)[:, None, None] * frequency[None, None, :]
    cosine = jnp.cos(angles)
    sine_part = jnp.sin(angles)
    first_half = values[..., :half_dim]
    second_half = values[..., half_dim:]
    return jnp.concatenate(
        [
            first_half * cosine - second_half * sine_part,
            second_half * cosine + first_half * sine_part,
        ],
        axis=-1,
    )


def attend(queries, fresh_kv, cache_keys, cache_values, lengths, q_gain, k_gain):
    batch_rows = queries.shape[0]
    kv_heads = cache_keys.shape[1]
    cache_len = cache_keys.shape[2]
    head_dim = cache_keys.shape[3]
    head_count = queries.shape[1] // head_dim
    group_size = head_count // kv_heads
    scaled_q = rotate(
        rms_scale(queries.reshape(batch_rows, head_count, head_dim), q_gain), lengths
    ).astype(jnp.bfloat16)
    fresh_keys = fresh_kv[:, : kv_heads * head_dim].reshape(batch_rows, kv_heads, head_dim)
    fresh_values = fresh_kv[:, kv_heads * head_dim :].reshape(batch_rows, kv_heads, head_dim)
    scaled_k = rotate(rms_scale(fresh_keys, k_gain), lengths).astype(jnp.bfloat16)
    grouped = scaled_q.reshape(batch_rows, kv_heads, group_size, head_dim)
    factor = head_dim ** (-0.5)
    old_scores = (
        jnp.einsum("rgqd,rgkd->rgqk", grouped, cache_keys, preferred_element_type=jnp.float32)
        * factor
    )
    new_scores = (
        jnp.einsum("rgqd,rgd->rgq", grouped, scaled_k, preferred_element_type=jnp.float32) * factor
    )
    visible = jnp.arange(cache_len, dtype=jnp.int32)[None, :] < lengths[:, None]
    old_scores = jnp.where(visible[:, None, None, :], old_scores, -jnp.inf)
    highest = jnp.maximum(jnp.max(old_scores, axis=-1), new_scores)
    old_weights = jnp.exp(old_scores - highest[..., None])
    new_weights = jnp.exp(new_scores - highest)
    denominator = jnp.sum(old_weights, axis=-1) + new_weights
    old_weights = (old_weights / denominator[..., None]).astype(jnp.bfloat16)
    new_weights = (new_weights / denominator).astype(jnp.bfloat16)
    mixture = jnp.einsum(
        "rgqk,rgkd->rgqd", old_weights, cache_values, preferred_element_type=jnp.float32
    )
    mixture = (
        mixture
        + new_weights.astype(jnp.float32)[..., None]
        * fresh_values.astype(jnp.float32)[:, :, None, :]
    )
    return mixture.reshape(batch_rows, head_count * head_dim).astype(jnp.bfloat16)


def expert_rows(inputs, gate_w, up_w, down_w):
    gate_part = jnp.dot(inputs, gate_w, preferred_element_type=jnp.float32)
    upper_part = jnp.dot(inputs, up_w, preferred_element_type=jnp.float32)
    activated = (jax.nn.silu(gate_part) * upper_part).astype(jnp.bfloat16)
    return jnp.dot(activated, down_w, preferred_element_type=jnp.float32)


def body(
    tokens,
    norm_gain,
    q_gain,
    k_gain,
    post_gain,
    w_query,
    w_keyvalue,
    w_out,
    cache_keys,
    cache_values,
    lengths,
    expert_ids,
    w_gate,
    w_up,
    w_down,
):
    normed = rms_scale(tokens, norm_gain).astype(jnp.bfloat16)
    query_width = w_query.shape[1]
    piece = lax.all_gather(normed, "dev", axis=0, tiled=True)
    joined = jnp.concatenate(
        [
            jnp.dot(piece, w_query, preferred_element_type=jnp.float32),
            jnp.dot(piece, w_keyvalue, preferred_element_type=jnp.float32),
        ],
        axis=1,
    )
    projected = joined.astype(jnp.bfloat16)
    queries, fresh_kv = (
        lax.all_to_all(projected[:, :query_width], "dev", split_axis=0, concat_axis=1, tiled=True),
        lax.all_to_all(projected[:, query_width:], "dev", split_axis=0, concat_axis=1, tiled=True),
    )
    mixture = attend(queries, fresh_kv, cache_keys, cache_values, lengths, q_gain, k_gain)
    head_rows = lax.all_to_all(mixture, "dev", split_axis=1, concat_axis=0, tiled=True)
    own_rows = tokens.shape[0]
    attended = lax.psum_scatter(
        jnp.dot(head_rows, w_out, preferred_element_type=jnp.float32).astype(jnp.bfloat16),
        "dev",
        scatter_dimension=0,
        tiled=True,
    ).astype(jnp.float32)
    hidden = tokens.astype(jnp.float32) + attended
    ready = rms_scale(hidden, post_gain).astype(jnp.bfloat16)
    picks = expert_ids.shape[1]
    group_count = lax.axis_size("grp")
    member_count = lax.axis_size("dev")
    expert_count = group_count * member_count
    capacity = min(own_rows, max(3, (own_rows * picks + expert_count - 1) // expert_count + 1))
    model_width = tokens.shape[1]
    flat_ids = expert_ids.reshape(own_rows * picks)
    order_index = jnp.arange(own_rows * picks, dtype=jnp.int32)
    earlier = (flat_ids[:, None] == flat_ids[None, :]) & (
        order_index[None, :] < order_index[:, None]
    )
    slot_index = jnp.sum(earlier.astype(jnp.int32), axis=1)
    position = (flat_ids * capacity + slot_index).reshape(own_rows, picks)
    buffer_rows = jnp.arange(expert_count * capacity, dtype=jnp.int32)
    placing = jnp.any(position[None, :, :] == buffer_rows[:, None, None], axis=2).astype(
        jnp.bfloat16
    )
    outgoing = jnp.dot(placing, ready, preferred_element_type=jnp.float32).astype(jnp.bfloat16)
    arrived = lax.all_to_all(
        outgoing.reshape(expert_count, capacity, model_width),
        ("grp", "dev"),
        split_axis=0,
        concat_axis=0,
        tiled=True,
    )
    arrived = arrived.reshape(expert_count * capacity, model_width)
    full_gate, full_up, full_down = (
        lax.all_gather(w_gate, "role", axis=2, tiled=True),
        lax.all_gather(w_up, "role", axis=2, tiled=True),
        lax.all_gather(w_down, "role", axis=1, tiled=True),
    )
    expert_out = expert_rows(arrived, full_gate[0], full_up[0], full_down[0]).astype(jnp.bfloat16)
    returned = lax.all_to_all(
        expert_out.reshape(expert_count, capacity, model_width),
        ("grp", "dev"),
        split_axis=0,
        concat_axis=0,
        tiled=True,
    )
    returned = returned.reshape(expert_count * capacity, model_width)
    selected = (
        jnp.take(returned, position.reshape(own_rows * picks), axis=0)
        .astype(jnp.float32)
        .reshape(own_rows, picks, model_width)
    )
    output = hidden + jnp.sum(selected, axis=1) / picks
    return output.astype(jnp.bfloat16)


def solution(mesh):
    return jax.shard_map(
        body,
        mesh=mesh,
        in_specs=(
            P(("role", "grp", "dev"), None),
            P(),
            P(),
            P(),
            P(),
            P(None, "dev"),
            P(None, "dev"),
            P("dev", None),
            P(("role", "grp", "dev"), None, None, None),
            P(("role", "grp", "dev"), None, None, None),
            P(("role", "grp", "dev")),
            P(("role", "grp", "dev"), None),
            P(("grp", "dev"), None, "role"),
            P(("grp", "dev"), None, "role"),
            P(("grp", "dev"), "role", None),
        ),
        out_specs=P(("role", "grp", "dev"), None),
        check_vma=False,
    )
```

profile of v0, /device:TPU:0, one launch (start us, length us, event | category | flops | bytes accessed | tf_op | source)
XLA Modules:
  0.0 189.6 jit_solution(13995234379125536499)
XLA Ops:
  7.4 1.2 fusion.26
  9.5 16.3 %all_gather.12 = bf16[96,2048]{1,0:T(8,128)(2,1)S(1)} all-gather(bf16[24,2048]{1,0:T(8,128)(2,1)S(1)} %fusion.28), channel_id=1, replica_groups=mesh['role'=2,'grp'=4,'dev'=4] {'dev'}, dimensions={0}, use_global_device_ids=true | all-gather | bytes 491520 | tf_op jit(solution)/shard_map/all_gather | solution.py:100
  25.8 2.2 %convolution_convert_fusion.3 = bf16[96,256]{1,0:T(8,128)(2,1)} fusion(bf16[96,2048]{1,0:T(8,128)(2,1)S(1)} %all_gather.12, bf16[2048,256]{1,0:T(8,128)(2,1)} %param.21), kind=kOutput, calls=%fused_computation.18 | convolution fusion | flops 100687872 | bytes 1490944 | tf_op jit(solution)/shard_map/dot_general | solution.py:104
  28.0 5.4 %all-to-all-start.1 = ((bf16[4,24,256]{2,1,0:T(8,128)(2,1)}), bf16[4,24,256]{2,1,0:T(8,128)(2,1)}, u32[]{:S(2)}, u32[]{:S(2)}) async-start(bf16[4,24,256]{2,1,0:T(8,128)(2,1)} %bitcast.56), calls=%async_computation.1 | async-start | bytes 98304 | tf_op jit(solution)/shard_map/all_to_all | solution.py:111
  34.0 3.7 %convolution_convert_fusion.2 = bf16[96,1024]{1,0:T(8,128)(2,1)} fusion(bf16[96,2048]{1,0:T(8,128)(2,1)S(1)} %all_gather.12, bf16[2048,1024]{1,0:T(8,128)(2,1)} %param.20), kind=kOutput, calls=%fused_computation.17 | convolution fusion | flops 402751488 | bytes 4784128 | tf_op jit(solution)/shard_map/dot_general | solution.py:103
  39.1 4.5 %all-to-all-start = ((bf16[4,24,1024]{2,1,0:T(8,128)(2,1)}), bf16[4,24,1024]{2,1,0:T(8,128)(2,1)S(1)}, u32[]{:S(2)}, u32[]{:S(2)}) async-start(bf16[4,24,1024]{2,1,0:T(8,128)(2,1)} %bitcast.54), calls=%async_computation | async-start | bytes 393216 | tf_op jit(solution)/shard_map/all_to_all | solution.py:110
  46.8 3.1 %all-to-all-done = bf16[4,24,1024]{2,1,0:T(8,128)(2,1)S(1)} async-done(((bf16[4,24,1024]{2,1,0:T(8,128)(2,1)}), bf16[4,24,1024]{2,1,0:T(8,128)(2,1)S(1)}, u32[]{:S(2)}, u32[]{:S(2)}) %all-to-all-start) | async-done | bytes 196640 | tf_op jit(solution)/shard_map/all_to_all | solution.py:110
  50.9 1.2 reshape.218
  55.3 1.9 fusion.46
  58.7 9.8 %all_to_all.58 = bf16[24,4,1024]{2,0,1:T(8,128)(2,1)S(1)} all-to-all(bf16[24,4,1024]{2,0,1:T(8,128)(2,1)S(1)} %copy.30), channel_id=1, replica_groups=mesh['role'=2,'grp'=4,'dev'=4] {'dev'}, dimensions={1} | all-to-all | bytes 393216 | tf_op jit(solution)/shard_map/all_to_all | solution.py:114
  68.5 3.7 %convolution_convert_fusion.1 = bf16[96,2048]{1,0:T(8,128)(2,1)} fusion(bf16[96,1024]{1,0:T(8,128)(2,1)S(1)} %bitcast.55, bf16[1024,2048]{1,0:T(8,128)(2,1)} %param.22), kind=kOutput, calls=%fused_computation.9 | convolution fusion | flops 402849792 | bytes 4784128 | tf_op jit(solution)/shard_map/dot_general | solution.py:117
  74.7 17.5 %reduce-scatter.2.cloned.1.call-done = bf16[24,2048]{1,0:T(8,128)(2,1)} async-done(((bf16[96,2048]{1,0:T(8,128)(2,1)}), bf16[24,2048]{1,0:T(8,128)(2,1)}) %reduce-scatter.2.cloned.1.call-update) | async-done | bytes 98320 | tf_op jit(solution)/shard_map/reduce_scatter | solution.py:116
  93.2 2.3 %convolution_convert_fusion = bf16[208,2048]{1,0:T(8,128)(2,1)} fusion(pred[208,24]{0,1:T(8,128)(4,1)S(1)} %fusion.34, bf16[24,2048]{1,0:T(8,128)(2,1)} %reduce-scatter.2.cloned.1.call-done, bf16[24,2048]{1,0:T(8,128)(2,1)S(1)} %copy-done.1, f32[2048]{0:T(1024)S(1)} %copy-done.5, f32[24]{0:T(128)S(1)} %add_rsqrt_fusion.2), kind=kOutput, calls=%fused_computation.8 | convolution fusion | flops 21168128 | bytes 1061856 | tf_op jit(solution)/shard_map/dot_general | solution.py:141
  95.5 2.5 %reshape.214 = bf16[16,13,2048]{2,1,0:T(8,128)(2,1)} reshape(bf16[208,2048]{1,0:T(8,128)(2,1)} %convolution_convert_fusion) | data formatting | bytes 1703936 | tf_op jit(solution)/shard_map/reshape | solution.py:143
  98.0 29.8 %all_to_all.59 = bf16[16,13,2048]{2,1,0:T(8,128)(2,1)} all-to-all(bf16[16,13,2048]{2,1,0:T(8,128)(2,1)} %reshape.214), channel_id=1, replica_groups=mesh['role'=2,'grp'=4,'dev'=4] {'grp','dev'}, dimensions={0} | all-to-all | bytes 1703936 | tf_op jit(solution)/shard_map/all_to_all | solution.py:142
  127.8 2.4 %reshape.215 = bf16[208,2048]{1,0:T(8,128)(2,1)} reshape(bf16[16,13,2048]{2,1,0:T(8,128)(2,1)} %all_to_all.59) | data formatting | bytes 1703936 | tf_op jit(solution)/shard_map/reshape | solution.py:149
  130.2 3.9 %fusion.4 = f32[208,768]{1,0:T(8,128)} fusion(bf16[208,2048]{1,0:T(8,128)(2,1)} %reshape.215, bf16[1,2048,768]{2,1,0:T(8,128)(2,1)} %all-gather.4.cloned.1.call-done), kind=kOutput, calls=%fused_computation.5 | convolution fusion | flops 654311424 | bytes 4636672 | tf_op jit(solution)/shard_map/dot_general | solution.py:75
  134.1 6.0 %fusion.6 = bf16[208,2048]{1,0:T(8,128)(2,1)} fusion(bf16[1,768,2048]{2,1,0:T(8,128)(2,1)} %all-gather.8.cloned.1.call-done, bf16[208,2048]{1,0:T(8,128)(2,1)} %reshape.215, bf16[1,2048,768]{2,1,0:T(8,128)(2,1)} %all-gather.6.cloned.1.call-done, f32[208,768]{1,0:T(8,128)} %fusion.4), kind=kOutput, calls=%fused_computation.7 | convolution fusion | flops 1310007296 | bytes 8634368 | tf_op jit(solution)/shard_map/dot_general | solution.py:78
  140.1 2.5 %reshape.216 = bf16[16,13,2048]{2,1,0:T(8,128)(2,1)} reshape(bf16[208,2048]{1,0:T(8,128)(2,1)} %fusion.6) | data formatting | bytes 1703936 | tf_op jit(solution)/shard_map/reshape | solution.py:157
  142.5 4.5 %all-to-all-start.4 = ((bf16[16,13,2048]{2,1,0:T(8,128)(2,1)}), bf16[16,13,2048]{2,1,0:T(8,128)(2,1)}, u32[]{:S(2)}, u32[]{:S(2)}) async-start(bf16[16,13,2048]{2,1,0:T(8,128)(2,1)} %reshape.216), calls=%async_computation.5 | async-start | bytes 2097152 | tf_op jit(solution)/shard_map/all_to_all | solution.py:156
  147.2 25.8 %all-to-all-done.4 = bf16[16,13,2048]{2,1,0:T(8,128)(2,1)} async-done(((bf16[16,13,2048]{2,1,0:T(8,128)(2,1)}), bf16[16,13,2048]{2,1,0:T(8,128)(2,1)}, u32[]{:S(2)}, u32[]{:S(2)}) %all-to-all-start.4) | async-done | bytes 852000 | tf_op jit(solution)/shard_map/all_to_all | solution.py:156
  173.0 2.5 %reshape.217 = bf16[208,2048]{1,0:T(8,128)(2,1)} reshape(bf16[16,13,2048]{2,1,0:T(8,128)(2,1)} %all-to-all-done.4) | data formatting | bytes 1703936 | tf_op jit(solution)/shard_map/reshape | solution.py:163
  175.5 4.1 %gather_fusion = bf16[192,2048]{1,0:T(8,128)(2,1)} fusion(bf16[208,2048]{1,0:T(8,128)(2,1)} %reshape.217, s32[1024]{0:T(1024)S(1)} %pad_clamp_fusion), kind=kCustom, calls=%fused_computation | custom fusion | bytes 1573632 | tf_op jit(solution)/shard_map/jit(_take)/gather | solution.py:165
  179.6 1.8 convert_reduce_fusion
  (69 shorter events, 16.1 us)
Async XLA Ops:
  7.4 47.9 %copy-start = (bf16[24,4,128,128]{3,2,1,0:T(8,128)(2,1)S(1)}, bf16[24,4,128,128]{3,2,1,0:T(8,128)(2,1)}, u32[]{:S(2)}) copy-start(bf16[24,4,128,128]{3,2,1,0:T(8,128)(2,1)} %param.23) | copy-start | bytes 9437188
  28.0 11.2 %all-to-all-start.1 = ((bf16[4,24,256]{2,1,0:T(8,128)(2,1)}), bf16[4,24,256]{2,1,0:T(8,128)(2,1)}, u32[]{:S(2)}, u32[]{:S(2)}) async-start(bf16[4,24,256]{2,1,0:T(8,128)(2,1)} %bitcast.56), calls=%async_computation.1 | async-start | bytes 98304 | tf_op jit(solution)/shard_map/all_to_all | solution.py:111
  37.8 12.1 %copy-start.3 = (f32[24,64]{1,0:T(8,128)}, f32[24,64]{1,0:T(8,128)S(1)}, u32[]{:S(2)}) copy-start(f32[24,64]{1,0:T(8,128)S(1)} %get-tuple-element.16) | copy-start | bytes 18436
  39.1 10.7 %all-to-all-start = ((bf16[4,24,1024]{2,1,0:T(8,128)(2,1)}), bf16[4,24,1024]{2,1,0:T(8,128)(2,1)S(1)}, u32[]{:S(2)}, u32[]{:S(2)}) async-start(bf16[4,24,1024]{2,1,0:T(8,128)(2,1)} %bitcast.54), calls=%async_computation | async-start | bytes 393216 | tf_op jit(solution)/shard_map/all_to_all | solution.py:110
  43.6 48.5 %reduce-scatter.2.cloned.1.call-start = ((), (), s32[]{:S(2)}) async-start(), calls=%async_computation.6 | async-start | bytes 491520 | tf_op jit(solution)/shard_map/reduce_scatter | solution.py:116
  53.1 4.5 %copy-start.4 = (f32[24,4,128]{2,1,0:T(4,128)S(1)}, f32[24,4,128]{2,1,0:T(4,128)}, u32[]{:S(2)}) copy-start(f32[24,4,128]{2,1,0:T(4,128)} %reshape.220) | copy-start | bytes 147460
  53.1 4.5 %copy-start.7 = (bf16[24,4,128,128]{3,2,1,0:T(8,128)(2,1)S(1)}, bf16[24,4,128,128]{3,2,1,0:T(8,128)(2,1)}, u32[]{:S(2)}) copy-start(bf16[24,4,128,128]{3,2,1,0:T(8,128)(2,1)} %param.24) | copy-start | bytes 9437188
  72.3 1.8 copy-start.6
  72.3 19.9 %copy-start.1 = (bf16[24,2048]{1,0:T(8,128)(2,1)S(1)}, bf16[24,2048]{1,0:T(8,128)(2,1)}, u32[]{:S(2)}) copy-start(bf16[24,2048]{1,0:T(8,128)(2,1)} %param.15) | copy-start | bytes 294916
  72.3 20.9 %copy-start.5 = (f32[2048]{0:T(1024)S(1)}, f32[2048]{0:T(1024)}, u32[]{:S(2)}) copy-start(f32[2048]{0:T(1024)} %param.19) | copy-start | bytes 24580
  72.3 57.9 %all-gather.4.cloned.1.call-start = ((), (), s32[]{:S(2)}) async-start(), calls=%async_computation.7 | async-start | bytes 4718592 | tf_op jit(solution)/shard_map/all_gather | solution.py:151
  72.9 61.2 %all-gather.6.cloned.1.call-start = ((), (), s32[]{:S(2)}) async-start(), calls=%async_computation.8 | async-start | bytes 4718592 | tf_op jit(solution)/shard_map/all_gather | solution.py:152
  73.5 60.6 %all-gather.8.cloned.1.call-start = ((), (), s32[]{:S(2)}) async-start(), calls=%async_computation.9 | async-start | bytes 4718592 | tf_op jit(solution)/shard_map/all_gather | solution.py:153
  142.5 30.5 %all-to-all-start.4 = ((bf16[16,13,2048]{2,1,0:T(8,128)(2,1)}), bf16[16,13,2048]{2,1,0:T(8,128)(2,1)}, u32[]{:S(2)}, u32[]{:S(2)}) async-start(bf16[16,13,2048]{2,1,0:T(8,128)(2,1)} %reshape.216), calls=%async_computation.5 | async-start | bytes 2097152 | tf_op jit(solution)/shard_map/all_to_all | solution.py:156
  175.5 5.9 %copy-start.2 = (bf16[24,2048]{1,0:T(8,128)(2,1)S(1)}, bf16[24,2048]{1,0:T(8,128)(2,1)}, u32[]{:S(2)}) copy-start(bf16[24,2048]{1,0:T(8,128)(2,1)} %reduce-scatter.2.cloned.1.call-done) | copy-start | bytes 294916
Sparse Core Ops, SparseCore 0:
  72.4 19.6 reduce-scatter.1
Sparse Core Ops, SparseCore 1:
  74.3 10.8 all-gather.3
  86.6 13.1 all-gather.5
  101.1 13.2 all-gather.7
where the time goes:
time: 191 us; the launch traced here: 190 us
  blocking collectives  55.9 us (29%)
  waiting for transfers between devices  48.6 us (25%)
  matrix products  25.6 us (13%)
  local copies, waits for them, and re-layouts  18 us (9%)
  between operations  15.3 us (8%)
  starting transfers between devices  14.5 us (8%)
  other arithmetic  11.7 us (6%)
    all_to_all x1, blocking collectives, body(): lax.all_to_all(outgoing.reshape(expert_count, capacity, model_width), ('g...  29.8 us
    all_to_all x1, waiting for transfers between devices, body(): lax.all_to_all(expert_out.reshape(expert_count, capacity, model_width), (...  25.8 us
    reduce_scatter x1, waiting for transfers between devices, body(): lax.psum_scatter(jnp.dot(head_rows, w_out, preferred_element_type=jnp.flo...  17.5 us
    all_gather x1, blocking collectives, body(): piece = lax.all_gather(normed, 'dev', axis=0, tiled=True)  16.3 us
    all_to_all x1, blocking collectives, body(): lax.all_to_all(mixture, 'dev', split_axis=1, concat_axis=0, tiled=True)  9.82 us
    dot_general x1, matrix products, expert_rows(): return jnp.dot(activated, down_w, preferred_element_type=jnp.float32)  6 us
    all_to_all x1, starting transfers between devices, body(): lax.all_to_all(projected[:, query_width:], 'dev', split_axis=0, concat_ax...  5.37 us
    all_to_all x1, starting transfers between devices, body(): lax.all_to_all(expert_out.reshape(expert_count, capacity, model_width), (...  4.51 us
  transfers between devices with their start and end apart: 7, of which 4 were waited for; matrix products, arithmetic and copies ran while one was open for 11% of the time, Pallas kernels for 0%

commit v1 on v0

--- a/solution.py
+++ b/solution.py
@@ -1,10 +1,323 @@
+import functools
+
 import jax
 import jax.numpy as jnp
 from jax import lax
+from jax.experimental import pallas as pl
+from jax.experimental.pallas import tpu as pltpu
 from jax.sharding import PartitionSpec as P
 
 epsilon = 1e-06
 rope_base = 1000000.0
+LANES = 128
+VMEM = pl.BlockSpec(memory_space=pltpu.VMEM)
+SMEM = pl.BlockSpec(memory_space=pltpu.SMEM)
+F32 = jnp.float32
+BF16 = jnp.bfloat16
+
+
+def call(kernel, outs, specs, args, scratch=(), cost=None, limit=None):
+    flops, moved = cost or (0, 0)
+    return pl.pallas_call(
+        kernel,
+        out_shape=[jax.ShapeDtypeStruct(shape, dtype) for shape, dtype in outs],
+        in_specs=list(specs),
+        out_specs=[VMEM] * len(outs),
+        scratch_shapes=list(scratch),
+        cost_estimate=pl.CostEstimate(flops=flops, bytes_accessed=moved, transcendentals=0),
+        compiler_params=pltpu.CompilerParams(vmem_limit_bytes=limit),
+    )(*args)
+
+
+def exchange(pieces, axis, size):
+    got = [pieces[0]]
+    for step in range(1, size):
+        got.append(lax.ppermute(pieces[step], axis, [(i, i ^ step) for i in range(size)]))
+    return got
+
+
+def rms(values, gain):
+    mean_square = jnp.mean(values * values, axis=-1, keepdims=True)
+    return values * lax.rsqrt(mean_square + epsilon) * gain
+
+
+def stack(refs):
+    return jnp.concatenate([ref[...].astype(F32) for ref in refs], axis=0)
+
+
+def project_kernel(count, *refs):
+    blocks, (gain, w_query, w_keyvalue, ids), outs = refs[:count], refs[count : count + 4], refs[count + 4 :]
+    rows = blocks[0].shape[0]
+    query_width = w_query.shape[1]
+    kv_width = w_keyvalue.shape[1]
+    normed = rms(stack(blocks), gain[...]).astype(BF16)
+    queries = jnp.dot(normed, w_query[...], preferred_element_type=F32)
+    fresh = jnp.dot(normed, w_keyvalue[...], preferred_element_type=F32)
+    for step in range(count):
+        own = slice(step * rows, (step + 1) * rows)
+        outs[step][:, :query_width] = queries[own].astype(BF16)
+        outs[step][:, query_width : query_width + kv_width] = fresh[own].astype(BF16)
+        outs[step][:, query_width + kv_width :] = ids[...]
+
+
+def attend_kernel(count, me_ref, *refs):
+    messages = refs[:count]
+    q_gain, k_gain, cosine, sine, bias, cache_keys, cache_values = refs[count : count + 7]
+    outs = refs[count + 7 : 2 * count + 7]
+    q_rot, k_rot, v_new, kv_all, mixed = refs[2 * count + 7 :]
+    me = me_ref[0]
+    rows, heads, places, dim = cache_keys.shape
+    group = q_rot.shape[1] // rows
+    query_width = group * dim
+    kv_width = kv_all.shape[2]
+    cos, sin = cosine[...], sine[...]
+
+    def turn(values, gain):
+        values = rms(values, gain)
+        return values * cos + pltpu.roll(values, dim // 2, 1) * sin
+
+    for step in range(count):
+        kv_all[me ^ step] = messages[step][:, query_width : query_width + kv_width].astype(F32)
+        for h in range(group):
+            piece = messages[step][:, h * dim : (h + 1) * dim].astype(F32)
+            q_rot[step, pl.ds(h, rows, stride=group), :] = turn(piece, q_gain[...])
+    for h in range(2 * heads):
+        column = h * dim
+        piece = kv_all[column // kv_width, :, column % kv_width : column % kv_width + dim]
+        if h < heads:
+            k_rot[h] = turn(piece, k_gain[...]).astype(BF16).astype(F32)
+        else:
+            v_new[h - heads] = piece
+    factor = dim ** (-0.5)
+    seen = bias[...][:, None, :]
+    for step in range(count):
+        head = me ^ step
+        query = q_rot[step].reshape(rows, group, dim).astype(BF16)
+        old = (
+            jnp.einsum("rqd,rkd->rqk", query, cache_keys[:, head], preferred_element_type=F32) * factor
+            + seen
+        )
+        new = jnp.sum(query.astype(F32) * k_rot[head][:, None, :], axis=-1, keepdims=True) * factor
+        highest = jnp.maximum(jnp.max(old, axis=-1, keepdims=True), new)
+        old = jnp.exp(old - highest)
+        new = jnp.exp(new - highest)
+        total = jnp.sum(old, axis=-1, keepdims=True) + new
+        old = (old / total).astype(BF16)
+        new = (new / total).astype(BF16).astype(F32)
+        out = jnp.einsum("rqk,rkd->rqd", old, cache_values[:, head], preferred_element_type=F32)
+        out = out + new * v_new[head][:, None, :]
+        mixed[...] = out.reshape(rows * group, dim)
+        for h in range(group):
+            outs[step][:, h * dim : (h + 1) * dim] = mixed[pl.ds(h, rows, stride=group), :].astype(BF16)
+
+
+def out_kernel(count, *refs):
+    blocks, w_out, outs = refs[:count], refs[count], refs[count + 1 :]
+    rows = blocks[0].shape[0]
+    partial = jnp.dot(stack(blocks).astype(BF16), w_out[...], preferred_element_type=F32)
+    for step in range(count):
+        outs[step][...] = partial[step * rows : (step + 1) * rows].astype(outs[step].dtype)
+
+
+def ready_kernel(count, *refs):
+    blocks, (tokens, gain), (hidden, ready) = refs[:count], refs[count : count + 2], refs[count + 2 :]
+    total = blocks[0][...]
+    for block in blocks[1:]:
+        total = total + block[...].astype(F32)
+    total = tokens[...].astype(F32) + total
+    hidden[...] = total
+    ready[...] = rms(total, gain[...]).astype(BF16)
+
+
+def route_kernel(count, groups, capacity, stride, where_ref, *refs):
+    ids, out = refs[:count], refs[count]
+    dev, grp = where_ref[0], where_ref[1]
+    table = stack(ids)
+    total = table.shape[0]
+    rows = total // count
+    lane = lax.broadcasted_iota(jnp.int32, (total, LANES), 1)
+    named = jnp.zeros((total, LANES), F32)
+    for step in range(groups):
+        expert = ((grp ^ step) * count + dev).astype(F32)
+        hit = jnp.max(jnp.where(table == expert, 1.0, 0.0), axis=1, keepdims=True)
+        named = jnp.where(lane == step, hit, named)
+    down = lax.broadcasted_iota(jnp.int32, (total, total), 0)
+    across = lax.broadcasted_iota(jnp.int32, (total, total), 1)
+    earlier = jnp.where((across < down) & (across // rows == down // rows), 1.0, 0.0)
+    rank = jnp.dot(earlier.astype(BF16), named.astype(BF16), preferred_element_type=F32)
+    source = (lax.broadcasted_iota(jnp.int32, (total, LANES), 0) // rows).astype(F32)
+    slot = rank + source * capacity + lane.astype(F32) * stride
+    place = lax.broadcasted_iota(jnp.int32, (total, groups * stride), 1).astype(F32)
+    chosen = jnp.zeros((total, groups * stride), F32)
+    for step in range(groups):
+        match = (place == slot[:, step : step + 1]) & (named[:, step : step + 1] > 0)
+        chosen = jnp.where(match, 1.0, chosen)
+    out[...] = chosen.astype(BF16)
+
+
+def pack_kernel(count, *refs):
+    blocks, choice, outs = refs[:count], refs[count], refs[count + 1 :]
+    stride = outs[0].shape[0]
+    packed = lax.dot_general(
+        choice[...], stack(blocks).astype(BF16), (((0,), (0,)), ((), ())), preferred_element_type=F32
+    )
+    for step, out in enumerate(outs):
+        out[...] = packed[step * stride : (step + 1) * stride].astype(BF16)
+
+
+def expert_kernel(groups, *refs):
+    blocks, weights, outs = refs[:groups], refs[groups : groups + 6], refs[groups + 6 :]
+    stride = outs[0].shape[0]
+    inputs = stack(blocks).astype(BF16)
+    total = None
+    for half in range(2):
+        gate, up, down = weights[3 * half : 3 * half + 3]
+        gated = jnp.dot(inputs, gate[...], preferred_element_type=F32)
+        upper = jnp.dot(inputs, up[...], preferred_element_type=F32)
+        active = (gated / (1.0 + jnp.exp(-gated)) * upper).astype(BF16)
+        part = jnp.dot(active, down[...], preferred_element_type=F32)
+        total = part if total is None else total + part
+    for step, out in enumerate(outs):
+        out[...] = total[step * stride : (step + 1) * stride].astype(BF16)
+
+
+def combine_kernel(groups, *refs):
+    blocks, choice, outs = refs[:groups], refs[groups], refs[groups + 1 :]
+    summed = jnp.dot(choice[...], stack(blocks).astype(BF16), preferred_element_type=F32)
+    rows = outs[0].shape[0]
+    for step, out in enumerate(outs):
+        out[...] = summed[step * rows : (step + 1) * rows].astype(out.dtype)
+
+
+def final_kernel(count, picks, *refs):
+    blocks, hidden, out = refs[:count], refs[count], refs[count + 1]
+    total = blocks[0][...]
+    for block in blocks[1:]:
+        total = total + block[...].astype(F32)
+    out[...] = (hidden[...] + total / picks).astype(BF16)
+
+
+def body(
+    tokens,
+    norm_gain,
+    q_gain,
+    k_gain,
+    post_gain,
+    w_query,
+    w_keyvalue,
+    w_out,
+    cache_keys,
+    cache_values,
+    lengths,
+    expert_ids,
+    w_gate,
+    w_up,
+    w_down,
+):
+    count, groups = lax.axis_size("dev"), lax.axis_size("grp")
+    rows, width = tokens.shape
+    picks = expert_ids.shape[1]
+    heads, places, dim = cache_keys.shape[1:]
+    query_width, kv_width = w_query.shape[1], w_keyvalue.shape[1]
+    group = query_width // dim
+    experts = count * groups
+    capacity = min(rows, max(3, (rows * picks + experts - 1) // experts + 1))
+    stride = -(-count * capacity // 8) * 8
+    dev, grp = lax.axis_index("dev"), lax.axis_index("grp")
+
+    swap = [(0, 1), (1, 0)]
+    own_weights = [w_gate[0], w_up[0], w_down[0]]
+    gathered = exchange([tokens] * count, "dev", count)
+    other_weights = [lax.ppermute(w, "role", swap) for w in own_weights]
+
+    ids = jnp.pad(expert_ids.astype(BF16), ((0, 0), (0, LANES - picks)), constant_values=-1)
+    frequency = rope_base ** (-jnp.arange(dim // 2, dtype=F32) / (dim // 2))
+    angles = lengths.astype(F32)[:, None] * frequency[None, :]
+    cosine, sine = jnp.cos(angles), jnp.sin(angles)
+    cosine = jnp.concatenate([cosine, cosine], axis=1)
+    sine = jnp.concatenate([-sine, sine], axis=1)
+    visible = jnp.arange(places, dtype=jnp.int32)[None, :] < lengths[:, None]
+    bias = jnp.where(visible, 0.0, -jnp.inf).astype(F32)
+
+    messages = call(
+        functools.partial(project_kernel, count),
+        [((rows, query_width + kv_width + LANES), BF16)] * count,
+        [VMEM] * (count + 4),
+        [*gathered, norm_gain.reshape(1, -1), w_query, w_keyvalue, ids],
+        limit=16 << 20,
+    )
+    messages = exchange(messages, "dev", count)
+    mixtures = call(
+        functools.partial(attend_kernel, count),
+        [((rows, query_width), BF16)] * count,
+        [SMEM] + [VMEM] * (count + 7),
+        [dev.reshape(1), *messages, q_gain.reshape(1, -1), k_gain.reshape(1, -1), cosine, sine, bias]
+        + [cache_keys, cache_values],
+        scratch=[
+            pltpu.VMEM((count, rows * group, dim), F32),
+            pltpu.VMEM((heads, rows, dim), F32),
+            pltpu.VMEM((heads, rows, dim), F32),
+            pltpu.VMEM((count, rows, kv_width), F32),
+            pltpu.VMEM((rows * group, dim), F32),
+        ],
+        limit=24 << 20,
+    )
+    [choice] = call(
+        functools.partial(route_kernel, count, groups, capacity, stride),
+        [((count * rows, groups * stride), BF16)],
+        [SMEM] + [VMEM] * count,
+        [jnp.stack([dev, grp])] + [m[:, query_width + kv_width :] for m in messages],
+        limit=8 << 20,
+    )
+    mixtures = exchange(mixtures, "dev", count)
+    partials = call(
+        functools.partial(out_kernel, count),
+        [((rows, width), F32)] + [((rows, width), BF16)] * (count - 1),
+        [VMEM] * (count + 1),
+        [*mixtures, w_out],
+        limit=16 << 20,
+    )
+    partials = exchange(partials, "dev", count)
+    hidden, ready = call(
+        functools.partial(ready_kernel, count),
+        [((rows, width), F32), ((rows, width), BF16)],
+        [VMEM] * (count + 2),
+        [*partials, tokens, post_gain.reshape(1, -1)],
+        limit=8 << 20,
+    )
+    ready = exchange([ready] * count, "dev", count)
+    packed = call(
+        functools.partial(pack_kernel, count),
+        [((stride, width), BF16)] * groups,
+        [VMEM] * (count + 1),
+        [*ready, choice],
+        limit=12 << 20,
+    )
+    packed = exchange(packed, "grp", groups)
+    results = call(
+        functools.partial(expert_kernel, groups),
+        [((stride, width), BF16)] * groups,
+        [VMEM] * (groups + 6),
+        [*packed, *own_weights, *other_weights],
+        limit=32 << 20,
+    )
+    results = exchange(results, "grp", groups)
+    sums = call(
+        functools.partial(combine_kernel, groups),
+        [((rows, width), F32)] + [((rows, width), BF16)] * (count - 1),
+        [VMEM] * (groups + 1),
+        [*results, choice],
+        limit=12 << 20,
+    )
+    sums = exchange(sums, "dev", count)
+    [output] = call(
+        functools.partial(final_kernel, count, picks),
+        [((rows, width), BF16)],
+        [VMEM] * (count + 1),
+        [*sums, hidden],
+        limit=8 << 20,
+    )
+    return output
 
 
 def rms_scale(values, gain):
@@ -78,7 +391,7 @@
     return jnp.dot(activated, down_w, preferred_element_type=jnp.float32)
 
 
-def body(
+def general_body(
     tokens,
     norm_gain,
     q_gain,
@@ -171,8 +484,16 @@
 
 
 def solution(mesh):
+    sizes = dict(mesh.shape)
+
+    def step(*args):
+        heads = args[8].shape[1]
+        powers = all(sizes[axis] & (sizes[axis] - 1) == 0 for axis in ("grp", "dev"))
+        fitted = sizes["dev"] == heads and sizes["role"] == 2 and powers
+        return (body if fitted else general_body)(*args)
+
     return jax.shard_map(
-        body,
+        step,
         mesh=mesh,
         in_specs=(
             P(("role", "grp", "dev"), None),

time: 191 us -> 120 us (0.63)
  blocking collectives: 55.9 us -> 0 us
  starting transfers between devices: 14.5 us -> 47.1 us
  matrix products: 25.6 us -> 0 us
  between operations: 15.3 us -> 0.2 us
  Pallas kernels: 0 us -> 13.7 us
  other arithmetic: 11.7 us -> 1.71 us
  local copies, waits for them, and re-layouts: 18 us -> 12.5 us
  waiting for transfers between devices: 48.6 us -> 43.9 us
    ppermute x0 -> x27, starting transfers between devices: none -> 47.1 us  [the longest x24 46.6 us: exchange(): lax.ppermute(pieces[step], axis, [(i, i ^ step) for i in range(size)])]
    ppermute x0 -> x27, waiting for transfers between devices: none -> 43.9 us  [the longest x24 43.9 us: exchange(): lax.ppermute(pieces[step], axis, [(i, i ^ step) for i in range(size)])]
    all_to_all x2 -> x0, blocking collectives: 39.7 us -> none  [the longest x1 29.8 us: body(): lax.all_to_all(outgoing.reshape(expert_count, capacity, model_width), ('g...]
    all_to_all x3 -> x0, waiting for transfers between devices: 29.5 us -> none  [the longest x1 25.8 us: body(): lax.all_to_all(expert_out.reshape(expert_count, capacity, model_width), (...]
    dot_general x9 -> x0, matrix products: 25.6 us -> none  [the longest x1 6 us: expert_rows(): return jnp.dot(activated, down_w, preferred_element_type=jnp.float32)]
    reduce_scatter x1 -> x0, waiting for transfers between devices: 17.5 us -> none  [body(): lax.psum_scatter(jnp.dot(head_rows, w_out, preferred_element_type=jnp.flo...]
    all_gather x1 -> x0, blocking collectives: 16.3 us -> none  [body(): piece = lax.all_gather(normed, 'dev', axis=0, tiled=True)]
    all_to_all x3 -> x0, starting transfers between devices: 14.4 us -> none  [the longest x1 5.37 us: body(): lax.all_to_all(projected[:, query_width:], 'dev', split_axis=0, concat_ax...]
  transfers between devices with their start and end apart: 7 -> 27, of which waited for: 4 -> 19; matrix products, arithmetic and copies ran while one was open for 11% -> 4% of each run, Pallas kernels for 0% -> 6%
where the time goes in v1:
time: 120 us; the launch traced here: 119 us
  starting transfers between devices  47.1 us (39%)
  waiting for transfers between devices  43.9 us (37%)
  Pallas kernels  13.7 us (11%)
  local copies, waits for them, and re-layouts  12.5 us (10%)
  other arithmetic  1.71 us (1%)
    ppermute x24, starting transfers between devices, exchange(): lax.ppermute(pieces[step], axis, [(i, i ^ step) for i in range(size)])  46.6 us
    ppermute x24, waiting for transfers between devices, exchange(): lax.ppermute(pieces[step], axis, [(i, i ^ step) for i in range(size)])  43.9 us
    pallas_call x9, Pallas kernels, call(): pl.pallas_call(kernel, out_shape=[jax.ShapeDtypeStruct(shape, dtype) for...  13.7 us
    unnamed x42, local copies, waits for them, and re-layouts  9.62 us
    slice x4, local copies, waits for them, and re-layouts, body(): m[:, query_width + kv_width:]  2.77 us
  transfers between devices with their start and end apart: 27, of which 19 were waited for; matrix products, arithmetic and copies ran while one was open for 4% of the time, Pallas kernels for 6%

profile of v1, /device:TPU:0, one launch (start us, length us, event | category | flops | bytes accessed | tf_op | source)
XLA Modules:
  0.0 119.1 jit_solution(11859119870236698421)
XLA Ops:
  0.0 5.1 %collective-permute-start.2 = (bf16[24,2048]{1,0:T(8,128)(2,1)}, bf16[24,2048]{1,0:T(8,128)(2,1)S(1)}, u32[]{:S(2)}, u32[]{:S(2)}) collective-permute-start(bf16[24,2048]{1,0:T(8,128)(2,1)} %refs_4_.3), channel_id=1, source_target_pairs={{0,3},{1,2},{2,1},{3,0},{4,7},{5,6},{6,5},{7,4},{8,11},{9,10},{10,... | collective-permute-start | bytes 294920 | tf_op jit(solution)/shard_map/ppermute | solution.py:35
  6.3 2.7 %collective-permute-done.2.refs_3_ = bf16[24,2048]{1,0:T(8,128)(2,1)S(1)} collective-permute-done((bf16[24,2048]{1,0:T(8,128)(2,1)}, bf16[24,2048]{1,0:T(8,128)(2,1)S(1)}, u32[]{:S(2)}, u32[]{:S(2)}) %collective-permute-start.2) | collective-permute-done | bytes 98336 | tf_op jit(solution)/shard_map/ppermute | solution.py:35
  9.0 4.0 %collective-permute-start = (bf16[24,2048]{1,0:T(8,128)(2,1)}, bf16[24,2048]{1,0:T(8,128)(2,1)S(1)}, u32[]{:S(2)}, u32[]{:S(2)}) collective-permute-start(bf16[24,2048]{1,0:T(8,128)(2,1)} %refs_4_.3), channel_id=1, source_target_pairs={{0,1},{1,0},{2,3},{3,2},{4,5},{5,4},{6,7},{7,6},{8,9},{9,8},{10,11... | collective-permute-start | bytes 294920 | tf_op jit(solution)/shard_map/ppermute | solution.py:35
  15.8 2.2 %copy-done = bf16[2048,1024]{1,0:T(8,128)(2,1)S(1)} copy-done((bf16[2048,1024]{1,0:T(8,128)(2,1)S(1)}, bf16[2048,1024]{1,0:T(8,128)(2,1)}, u32[]{:S(2)}) %copy-start) | copy-done | bytes 4194328
  23.7 2.0 %collective-permute-start.3 = (bf16[24,1408]{1,0:T(8,128)(2,1)}, bf16[24,1408]{1,0:T(8,128)(2,1)S(1)}, u32[]{:S(2)}, u32[]{:S(2)}) collective-permute-start(bf16[24,1408]{1,0:T(8,128)(2,1)} %get-tuple-element.32), channel_id=1, source_target_pairs={{0,1},{1,0},{2,3},{3,2},{4,5},{5,4},{6,7},{7,6},{8,9},{9,8},{10,11... | collective-permute-start | bytes 202760 | tf_op jit(solution)/shard_map/ppermute | solution.py:35
  28.2 2.8 %collective-permute-start.5 = (bf16[24,1408]{1,0:T(8,128)(2,1)}, bf16[24,1408]{1,0:T(8,128)(2,1)S(1)}, u32[]{:S(2)}, u32[]{:S(2)}) collective-permute-start(bf16[24,1408]{1,0:T(8,128)(2,1)} %copy-done.18), channel_id=1, source_target_pairs={{0,3},{1,2},{2,1},{3,0},{4,7},{5,6},{6,5},{7,4},{8,11},{9,10},{10,... | collective-permute-start | bytes 202760 | tf_op jit(solution)/shard_map/ppermute | solution.py:35
  32.6 2.1 %collective-permute-done.5.refs_3_ = bf16[24,1408]{1,0:T(8,128)(2,1)S(1)} collective-permute-done((bf16[24,1408]{1,0:T(8,128)(2,1)}, bf16[24,1408]{1,0:T(8,128)(2,1)S(1)}, u32[]{:S(2)}, u32[]{:S(2)}) %collective-permute-start.5) | collective-permute-done | bytes 67616 | tf_op jit(solution)/shard_map/ppermute | solution.py:35
  36.6 3.2 %shard_map.146 = (bf16[24,1024]{1,0:T(8,128)(2,1)S(1)}, bf16[24,1024]{1,0:T(8,128)(2,1)S(1)}, bf16[24,1024]{1,0:T(8,128)(2,1)S(1)}, bf16[24,1024]{1,0:T(8,128)(2,1)S(1)}) custom-call(s32[1]{0:T(128)} %bitcast.me_ref, bf16[24,1408]{1,0:T(8,128)(2,1)S(1)} %get-tuple-element.31.refs_0_, bf16[24,1408]{1,0:T(8,128)(2,1)S(1)} %collective-permute-done.3.refs_1_, ...), custom_call_target="tpu_custom_call" | custom-call | tf_op jit(solution)/shard_map/pallas_call | solution.py:21
  40.9 2.2 %collective-permute-start.7 = (bf16[24,1024]{1,0:T(8,128)(2,1)S(1)}, bf16[24,1024]{1,0:T(8,128)(2,1)S(1)}, u32[]{:S(2)}, u32[]{:S(2)}) collective-permute-start(bf16[24,1024]{1,0:T(8,128)(2,1)S(1)} %get-tuple-element.37), channel_id=1, source_target_pairs={{0,2},{1,3},{2,0},{3,1},{4,6},{5,7},{6,4},{7,5},{8,10},{9,11},{10,... | collective-permute-start | bytes 147464 | tf_op jit(solution)/shard_map/ppermute | solution.py:35
  43.9 2.7 %collective-permute-start.8 = (bf16[24,1024]{1,0:T(8,128)(2,1)S(1)}, bf16[24,1024]{1,0:T(8,128)(2,1)S(1)}, u32[]{:S(2)}, u32[]{:S(2)}) collective-permute-start(bf16[24,1024]{1,0:T(8,128)(2,1)S(1)} %get-tuple-element.38), channel_id=1, source_target_pairs={{0,3},{1,2},{2,1},{3,0},{4,7},{5,6},{6,5},{7,4},{8,11},{9,10},{10,... | collective-permute-start | bytes 147464 | tf_op jit(solution)/shard_map/ppermute | solution.py:35
  46.7 3.3 %collective-permute-done.8.refs_3_ = bf16[24,1024]{1,0:T(8,128)(2,1)S(1)} collective-permute-done((bf16[24,1024]{1,0:T(8,128)(2,1)S(1)}, bf16[24,1024]{1,0:T(8,128)(2,1)S(1)}, u32[]{:S(2)}, u32[]{:S(2)}) %collective-permute-start.8) | collective-permute-done | bytes 49184 | tf_op jit(solution)/shard_map/ppermute | solution.py:35
  51.5 2.9 %collective-permute-start.10 = (bf16[24,2048]{1,0:T(8,128)(2,1)S(1)}, bf16[24,2048]{1,0:T(8,128)(2,1)S(1)}, u32[]{:S(2)}, u32[]{:S(2)}) collective-permute-start(bf16[24,2048]{1,0:T(8,128)(2,1)S(1)} %get-tuple-element.41), channel_id=1, source_target_pairs={{0,2},{1,3},{2,0},{3,1},{4,6},{5,7},{6,4},{7,5},{8,10},{9,11},{10,... | collective-permute-start | bytes 294920 | tf_op jit(solution)/shard_map/ppermute | solution.py:35
  55.7 2.7 %collective-permute-start.11 = (bf16[24,2048]{1,0:T(8,128)(2,1)S(1)}, bf16[24,2048]{1,0:T(8,128)(2,1)S(1)}, u32[]{:S(2)}, u32[]{:S(2)}) collective-permute-start(bf16[24,2048]{1,0:T(8,128)(2,1)S(1)} %get-tuple-element.42), channel_id=1, source_target_pairs={{0,3},{1,2},{2,1},{3,0},{4,7},{5,6},{6,5},{7,4},{8,11},{9,10},{10,... | collective-permute-start | bytes 294920 | tf_op jit(solution)/shard_map/ppermute | solution.py:35
  58.9 3.4 %collective-permute-done.11.refs_3_ = bf16[24,2048]{1,0:T(8,128)(2,1)S(1)} collective-permute-done((bf16[24,2048]{1,0:T(8,128)(2,1)S(1)}, bf16[24,2048]{1,0:T(8,128)(2,1)S(1)}, u32[]{:S(2)}, u32[]{:S(2)}) %collective-permute-start.11) | collective-permute-done | bytes 98336 | tf_op jit(solution)/shard_map/ppermute | solution.py:35
  62.5 3.3 %collective-permute-start.14 = (bf16[24,2048]{1,0:T(8,128)(2,1)S(1)}, bf16[24,2048]{1,0:T(8,128)(2,1)S(1)}, u32[]{:S(2)}, u32[]{:S(2)}) collective-permute-start(bf16[24,2048]{1,0:T(8,128)(2,1)S(1)} %get-tuple-element.43.refs_0_), channel_id=1, source_target_pairs={{0,3},{1,2},{2,1},{3,0},{4,7},{5,6},{6,5},{7,4},{8,11},{9,10},{10,... | collective-permute-start | bytes 294920 | tf_op jit(solution)/shard_map/ppermute | solution.py:35
  66.4 2.7 %collective-permute-done.14.refs_3_ = bf16[24,2048]{1,0:T(8,128)(2,1)S(1)} collective-permute-done((bf16[24,2048]{1,0:T(8,128)(2,1)S(1)}, bf16[24,2048]{1,0:T(8,128)(2,1)S(1)}, u32[]{:S(2)}, u32[]{:S(2)}) %collective-permute-start.14) | collective-permute-done | bytes 98336 | tf_op jit(solution)/shard_map/ppermute | solution.py:35
  78.3 3.0 %collective-permute-done.15.refs_1_ = bf16[56,2048]{1,0:T(8,128)(2,1)S(1)} collective-permute-done((bf16[56,2048]{1,0:T(8,128)(2,1)S(1)}, bf16[56,2048]{1,0:T(8,128)(2,1)S(1)}, u32[]{:S(2)}, u32[]{:S(2)}) %collective-permute-start.15) | collective-permute-done | bytes 229408 | tf_op jit(solution)/shard_map/ppermute | solution.py:35
  81.3 2.5 %collective-permute-start.17 = (bf16[56,2048]{1,0:T(8,128)(2,1)S(1)}, bf16[56,2048]{1,0:T(8,128)(2,1)S(1)}, u32[]{:S(2)}, u32[]{:S(2)}) collective-permute-start(bf16[56,2048]{1,0:T(8,128)(2,1)S(1)} %get-tuple-element.47), channel_id=1, source_target_pairs={{0,12},{4,8},{8,4},{12,0},{1,13},{5,9},{9,5},{13,1},{2,14},{6,10},... | collective-permute-start | bytes 688136 | tf_op jit(solution)/shard_map/ppermute | solution.py:35
  83.8 7.0 %collective-permute-done.17.refs_3_ = bf16[56,2048]{1,0:T(8,128)(2,1)S(1)} collective-permute-done((bf16[56,2048]{1,0:T(8,128)(2,1)S(1)}, bf16[56,2048]{1,0:T(8,128)(2,1)S(1)}, u32[]{:S(2)}, u32[]{:S(2)}) %collective-permute-start.17) | collective-permute-done | bytes 229408 | tf_op jit(solution)/shard_map/ppermute | solution.py:35
  92.3 5.5 %shard_map.151 = (bf16[56,2048]{1,0:T(8,128)(2,1)S(1)}, bf16[56,2048]{1,0:T(8,128)(2,1)S(1)}, bf16[56,2048]{1,0:T(8,128)(2,1)S(1)}, bf16[56,2048]{1,0:T(8,128)(2,1)S(1)}) custom-call(bf16[56,2048]{1,0:T(8,128)(2,1)S(1)} %get-tuple-element.44.refs_0_, bf16[56,2048]{1,0:T(8,128)(2,1)S(1)} %collective-permute-done.15.refs_1_, ...), custom_call_target="tpu_custom_call" | custom-call | tf_op jit(solution)/shard_map/pallas_call | solution.py:21
  101.3 2.5 %collective-permute-done.21.refs_1_ = bf16[56,2048]{1,0:T(8,128)(2,1)S(1)} collective-permute-done((bf16[56,2048]{1,0:T(8,128)(2,1)S(1)}, bf16[56,2048]{1,0:T(8,128)(2,1)S(1)}, u32[]{:S(2)}, u32[]{:S(2)}) %collective-permute-start.21) | collective-permute-done | bytes 229408 | tf_op jit(solution)/shard_map/ppermute | solution.py:35
  103.8 3.0 %collective-permute-done.22.refs_2_ = bf16[56,2048]{1,0:T(8,128)(2,1)S(1)} collective-permute-done((bf16[56,2048]{1,0:T(8,128)(2,1)S(1)}, bf16[56,2048]{1,0:T(8,128)(2,1)S(1)}, u32[]{:S(2)}, u32[]{:S(2)}) %collective-permute-start.22) | collective-permute-done | bytes 229408 | tf_op jit(solution)/shard_map/ppermute | solution.py:35
  108.9 3.1 %collective-permute-start.25 = (bf16[24,2048]{1,0:T(8,128)(2,1)S(1)}, bf16[24,2048]{1,0:T(8,128)(2,1)S(1)}, u32[]{:S(2)}, u32[]{:S(2)}) collective-permute-start(bf16[24,2048]{1,0:T(8,128)(2,1)S(1)} %get-tuple-element.54), channel_id=1, source_target_pairs={{0,2},{1,3},{2,0},{3,1},{4,6},{5,7},{6,4},{7,5},{8,10},{9,11},{10,... | collective-permute-start | bytes 294920 | tf_op jit(solution)/shard_map/ppermute | solution.py:35
  114.6 3.8 %collective-permute-done.26.refs_3_ = bf16[24,2048]{1,0:T(8,128)(2,1)S(1)} collective-permute-done((bf16[24,2048]{1,0:T(8,128)(2,1)S(1)}, bf16[24,2048]{1,0:T(8,128)(2,1)S(1)}, u32[]{:S(2)}, u32[]{:S(2)}) %collective-permute-start.26) | collective-permute-done | bytes 98336 | tf_op jit(solution)/shard_map/ppermute | solution.py:35
  (94 shorter events, 41.4 us)
Async XLA Ops:
  0.0 9.0 %collective-permute-start.2 = (bf16[24,2048]{1,0:T(8,128)(2,1)}, bf16[24,2048]{1,0:T(8,128)(2,1)S(1)}, u32[]{:S(2)}, u32[]{:S(2)}) collective-permute-start(bf16[24,2048]{1,0:T(8,128)(2,1)} %refs_4_.3), channel_id=1, source_target_pairs={{0,3},{1,2},{2,1},{3,0},{4,7},{5,6},{6,5},{7,4},{8,11},{9,10},{10,... | collective-permute-start | bytes 294920 | tf_op jit(solution)/shard_map/ppermute | solution.py:35
  5.1 8.8 %collective-permute-start.1 = (bf16[24,2048]{1,0:T(8,128)(2,1)}, bf16[24,2048]{1,0:T(8,128)(2,1)S(1)}, u32[]{:S(2)}, u32[]{:S(2)}) collective-permute-start(bf16[24,2048]{1,0:T(8,128)(2,1)} %refs_4_.3), channel_id=1, source_target_pairs={{0,2},{1,3},{2,0},{3,1},{4,6},{5,7},{6,4},{7,5},{8,10},{9,11},{10,... | collective-permute-start | bytes 294920 | tf_op jit(solution)/shard_map/ppermute | solution.py:35
  5.1 85.7 %collective-permute-start.18 = (bf16[2048,384]{1,0:T(8,128)(2,1)}, bf16[2048,384]{1,0:T(8,128)(2,1)}, u32[]{:S(2)}, u32[]{:S(2)}) collective-permute-start(bf16[2048,384]{1,0:T(8,128)(2,1)} %bitcast.9), channel_id=1, source_target_pairs={{0,16},{16,0},{1,17},{17,1},{2,18},{18,2},{3,19},{19,3},{4,20},{20... | collective-permute-start | bytes 4718600 | tf_op jit(solution)/shard_map/ppermute | solution.py:231
  5.1 85.7 %collective-permute-start.19 = (bf16[2048,384]{1,0:T(8,128)(2,1)}, bf16[2048,384]{1,0:T(8,128)(2,1)}, u32[]{:S(2)}, u32[]{:S(2)}) collective-permute-start(bf16[2048,384]{1,0:T(8,128)(2,1)} %bitcast.11), channel_id=1, source_target_pairs={{0,16},{16,0},{1,17},{17,1},{2,18},{18,2},{3,19},{19,3},{4,20},{20... | collective-permute-start | bytes 4718600 | tf_op jit(solution)/shard_map/ppermute | solution.py:231
  5.6 85.2 %collective-permute-start.20 = (bf16[384,2048]{1,0:T(8,128)(2,1)}, bf16[384,2048]{1,0:T(8,128)(2,1)}, u32[]{:S(2)}, u32[]{:S(2)}) collective-permute-start(bf16[384,2048]{1,0:T(8,128)(2,1)} %bitcast.13), channel_id=1, source_target_pairs={{0,16},{16,0},{1,17},{17,1},{2,18},{18,2},{3,19},{19,3},{4,20},{20... | collective-permute-start | bytes 4718600 | tf_op jit(solution)/shard_map/ppermute | solution.py:231
  9.0 6.8 %collective-permute-start = (bf16[24,2048]{1,0:T(8,128)(2,1)}, bf16[24,2048]{1,0:T(8,128)(2,1)S(1)}, u32[]{:S(2)}, u32[]{:S(2)}) collective-permute-start(bf16[24,2048]{1,0:T(8,128)(2,1)} %refs_4_.3), channel_id=1, source_target_pairs={{0,1},{1,0},{2,3},{3,2},{4,5},{5,4},{6,7},{7,6},{8,9},{9,8},{10,11... | collective-permute-start | bytes 294920 | tf_op jit(solution)/shard_map/ppermute | solution.py:35
  25.8 6.7 %collective-permute-start.4 = (bf16[24,1408]{1,0:T(8,128)(2,1)}, bf16[24,1408]{1,0:T(8,128)(2,1)S(1)}, u32[]{:S(2)}, u32[]{:S(2)}) collective-permute-start(bf16[24,1408]{1,0:T(8,128)(2,1)} %copy-done.19), channel_id=1, source_target_pairs={{0,2},{1,3},{2,0},{3,1},{4,6},{5,7},{6,4},{7,5},{8,10},{9,11},{10,... | collective-permute-start | bytes 202760 | tf_op jit(solution)/shard_map/ppermute | solution.py:35
  28.2 6.4 %collective-permute-start.5 = (bf16[24,1408]{1,0:T(8,128)(2,1)}, bf16[24,1408]{1,0:T(8,128)(2,1)S(1)}, u32[]{:S(2)}, u32[]{:S(2)}) collective-permute-start(bf16[24,1408]{1,0:T(8,128)(2,1)} %copy-done.18), channel_id=1, source_target_pairs={{0,3},{1,2},{2,1},{3,0},{4,7},{5,6},{6,5},{7,4},{8,11},{9,10},{10,... | collective-permute-start | bytes 202760 | tf_op jit(solution)/shard_map/ppermute | solution.py:35
  40.9 5.7 %collective-permute-start.7 = (bf16[24,1024]{1,0:T(8,128)(2,1)S(1)}, bf16[24,1024]{1,0:T(8,128)(2,1)S(1)}, u32[]{:S(2)}, u32[]{:S(2)}) collective-permute-start(bf16[24,1024]{1,0:T(8,128)(2,1)S(1)} %get-tuple-element.37), channel_id=1, source_target_pairs={{0,2},{1,3},{2,0},{3,1},{4,6},{5,7},{6,4},{7,5},{8,10},{9,11},{10,... | collective-permute-start | bytes 147464 | tf_op jit(solution)/shard_map/ppermute | solution.py:35
  43.9 6.1 %collective-permute-start.8 = (bf16[24,1024]{1,0:T(8,128)(2,1)S(1)}, bf16[24,1024]{1,0:T(8,128)(2,1)S(1)}, u32[]{:S(2)}, u32[]{:S(2)}) collective-permute-start(bf16[24,1024]{1,0:T(8,128)(2,1)S(1)} %get-tuple-element.38), channel_id=1, source_target_pairs={{0,3},{1,2},{2,1},{3,0},{4,7},{5,6},{6,5},{7,4},{8,11},{9,10},{10,... | collective-permute-start | bytes 147464 | tf_op jit(solution)/shard_map/ppermute | solution.py:35
  50.8 4.9 %collective-permute-start.9 = (bf16[24,2048]{1,0:T(8,128)(2,1)S(1)}, bf16[24,2048]{1,0:T(8,128)(2,1)S(1)}, u32[]{:S(2)}, u32[]{:S(2)}) collective-permute-start(bf16[24,2048]{1,0:T(8,128)(2,1)S(1)} %get-tuple-element.40), channel_id=1, source_target_pairs={{0,1},{1,0},{2,3},{3,2},{4,5},{5,4},{6,7},{7,6},{8,9},{9,8},{10,11... | collective-permute-start | bytes 294920 | tf_op jit(solution)/shard_map/ppermute | solution.py:35
  51.5 7.4 %collective-permute-start.10 = (bf16[24,2048]{1,0:T(8,128)(2,1)S(1)}, bf16[24,2048]{1,0:T(8,128)(2,1)S(1)}, u32[]{:S(2)}, u32[]{:S(2)}) collective-permute-start(bf16[24,2048]{1,0:T(8,128)(2,1)S(1)} %get-tuple-element.41), channel_id=1, source_target_pairs={{0,2},{1,3},{2,0},{3,1},{4,6},{5,7},{6,4},{7,5},{8,10},{9,11},{10,... | collective-permute-start | bytes 294920 | tf_op jit(solution)/shard_map/ppermute | solution.py:35
  55.7 6.6 %collective-permute-start.11 = (bf16[24,2048]{1,0:T(8,128)(2,1)S(1)}, bf16[24,2048]{1,0:T(8,128)(2,1)S(1)}, u32[]{:S(2)}, u32[]{:S(2)}) collective-permute-start(bf16[24,2048]{1,0:T(8,128)(2,1)S(1)} %get-tuple-element.42), channel_id=1, source_target_pairs={{0,3},{1,2},{2,1},{3,0},{4,7},{5,6},{6,5},{7,4},{8,11},{9,10},{10,... | collective-permute-start | bytes 294920 | tf_op jit(solution)/shard_map/ppermute | solution.py:35
  62.5 6.6 %collective-permute-start.14 = (bf16[24,2048]{1,0:T(8,128)(2,1)S(1)}, bf16[24,2048]{1,0:T(8,128)(2,1)S(1)}, u32[]{:S(2)}, u32[]{:S(2)}) collective-permute-start(bf16[24,2048]{1,0:T(8,128)(2,1)S(1)} %get-tuple-element.43.refs_0_), channel_id=1, source_target_pairs={{0,3},{1,2},{2,1},{3,0},{4,7},{5,6},{6,5},{7,4},{8,11},{9,10},{10,... | collective-permute-start | bytes 294920 | tf_op jit(solution)/shard_map/ppermute | solution.py:35
  65.8 9.0 %collective-permute-start.13 = (bf16[24,2048]{1,0:T(8,128)(2,1)S(1)}, bf16[24,2048]{1,0:T(8,128)(2,1)S(1)}, u32[]{:S(2)}, u32[]{:S(2)}) collective-permute-start(bf16[24,2048]{1,0:T(8,128)(2,1)S(1)} %get-tuple-element.43.refs_0_), channel_id=1, source_target_pairs={{0,2},{1,3},{2,0},{3,1},{4,6},{5,7},{6,4},{7,5},{8,10},{9,11},{10,... | collective-permute-start | bytes 294920 | tf_op jit(solution)/shard_map/ppermute | solution.py:35
  69.1 5.8 %collective-permute-start.12 = (bf16[24,2048]{1,0:T(8,128)(2,1)S(1)}, bf16[24,2048]{1,0:T(8,128)(2,1)S(1)}, u32[]{:S(2)}, u32[]{:S(2)}) collective-permute-start(bf16[24,2048]{1,0:T(8,128)(2,1)S(1)} %get-tuple-element.43.refs_0_), channel_id=1, source_target_pairs={{0,1},{1,0},{2,3},{3,2},{4,5},{5,4},{6,7},{7,6},{8,9},{9,8},{10,11... | collective-permute-start | bytes 294920 | tf_op jit(solution)/shard_map/ppermute | solution.py:35
  75.3 6.1 %collective-permute-start.15 = (bf16[56,2048]{1,0:T(8,128)(2,1)S(1)}, bf16[56,2048]{1,0:T(8,128)(2,1)S(1)}, u32[]{:S(2)}, u32[]{:S(2)}) collective-permute-start(bf16[56,2048]{1,0:T(8,128)(2,1)S(1)} %get-tuple-element.45), channel_id=1, source_target_pairs={{0,4},{4,0},{8,12},{12,8},{1,5},{5,1},{9,13},{13,9},{2,6},{6,2},{1... | collective-permute-start | bytes 688136 | tf_op jit(solution)/shard_map/ppermute | solution.py:35
  76.8 7.0 %collective-permute-start.16 = (bf16[56,2048]{1,0:T(8,128)(2,1)S(1)}, bf16[56,2048]{1,0:T(8,128)(2,1)S(1)}, u32[]{:S(2)}, u32[]{:S(2)}) collective-permute-start(bf16[56,2048]{1,0:T(8,128)(2,1)S(1)} %get-tuple-element.46), channel_id=1, source_target_pairs={{0,8},{4,12},{8,0},{12,4},{1,9},{5,13},{9,1},{13,5},{2,10},{6,14},... | collective-permute-start | bytes 688136 | tf_op jit(solution)/shard_map/ppermute | solution.py:35
  81.3 9.5 %collective-permute-start.17 = (bf16[56,2048]{1,0:T(8,128)(2,1)S(1)}, bf16[56,2048]{1,0:T(8,128)(2,1)S(1)}, u32[]{:S(2)}, u32[]{:S(2)}) collective-permute-start(bf16[56,2048]{1,0:T(8,128)(2,1)S(1)} %get-tuple-element.47), channel_id=1, source_target_pairs={{0,12},{4,8},{8,4},{12,0},{1,13},{5,9},{9,5},{13,1},{2,14},{6,10},... | collective-permute-start | bytes 688136 | tf_op jit(solution)/shard_map/ppermute | solution.py:35
  97.7 6.1 %collective-permute-start.21 = (bf16[56,2048]{1,0:T(8,128)(2,1)S(1)}, bf16[56,2048]{1,0:T(8,128)(2,1)S(1)}, u32[]{:S(2)}, u32[]{:S(2)}) collective-permute-start(bf16[56,2048]{1,0:T(8,128)(2,1)S(1)} %get-tuple-element.49), channel_id=1, source_target_pairs={{0,4},{4,0},{8,12},{12,8},{1,5},{5,1},{9,13},{13,9},{2,6},{6,2},{1... | collective-permute-start | bytes 688136 | tf_op jit(solution)/shard_map/ppermute | solution.py:35
  99.2 7.6 %collective-permute-start.22 = (bf16[56,2048]{1,0:T(8,128)(2,1)S(1)}, bf16[56,2048]{1,0:T(8,128)(2,1)S(1)}, u32[]{:S(2)}, u32[]{:S(2)}) collective-permute-start(bf16[56,2048]{1,0:T(8,128)(2,1)S(1)} %get-tuple-element.50), channel_id=1, source_target_pairs={{0,8},{4,12},{8,0},{12,4},{1,9},{5,13},{9,1},{13,5},{2,10},{6,14},... | collective-permute-start | bytes 688136 | tf_op jit(solution)/shard_map/ppermute | solution.py:35
  100.8 6.9 %collective-permute-start.23 = (bf16[56,2048]{1,0:T(8,128)(2,1)S(1)}, bf16[56,2048]{1,0:T(8,128)(2,1)S(1)}, u32[]{:S(2)}, u32[]{:S(2)}) collective-permute-start(bf16[56,2048]{1,0:T(8,128)(2,1)S(1)} %get-tuple-element.51), channel_id=1, source_target_pairs={{0,12},{4,8},{8,4},{12,0},{1,13},{5,9},{9,5},{13,1},{2,14},{6,10},... | collective-permute-start | bytes 688136 | tf_op jit(solution)/shard_map/ppermute | solution.py:35
  108.9 5.7 %collective-permute-start.25 = (bf16[24,2048]{1,0:T(8,128)(2,1)S(1)}, bf16[24,2048]{1,0:T(8,128)(2,1)S(1)}, u32[]{:S(2)}, u32[]{:S(2)}) collective-permute-start(bf16[24,2048]{1,0:T(8,128)(2,1)S(1)} %get-tuple-element.54), channel_id=1, source_target_pairs={{0,2},{1,3},{2,0},{3,1},{4,6},{5,7},{6,4},{7,5},{8,10},{9,11},{10,... | collective-permute-start | bytes 294920 | tf_op jit(solution)/shard_map/ppermute | solution.py:35
  112.0 6.4 %collective-permute-start.26 = (bf16[24,2048]{1,0:T(8,128)(2,1)S(1)}, bf16[24,2048]{1,0:T(8,128)(2,1)S(1)}, u32[]{:S(2)}, u32[]{:S(2)}) collective-permute-start(bf16[24,2048]{1,0:T(8,128)(2,1)S(1)} %get-tuple-element.55), channel_id=1, source_target_pairs={{0,3},{1,2},{2,1},{3,0},{4,7},{5,6},{6,5},{7,4},{8,11},{9,10},{10,... | collective-permute-start | bytes 294920 | tf_op jit(solution)/shard_map/ppermute | solution.py:35
  (24 other events, 229.1 us)
